TPU v7x, 32 devices: a whole 2x2x4 slice. The times are simulated.
32 devices in a mesh: gx: 2 (over y), gy: 4 (over x, core), gz: 4 (over z).
Axes of the slice: x: 2, y: 2, z: 4, core: 2. Of those that a mesh axis runs over, the one named last changes fastest.
Arguments:
- midpoints: float32 [3, 2, 4, 4, 1024], P(None, 'gx', 'gy', 'gz'), may hold values from 0 to 1
- line_vectors: float32 [3, 2, 4, 4, 1024], P(None, 'gx', 'gy', 'gz'), may hold values from -0.085 to 0.085
- burgers: float32 [3, 2, 4, 4, 1024], P(None, 'gx', 'gy', 'gz'), may hold values from -1.7 to 1.7
- live_mask: int32 [2, 4, 4, 1024], P('gx', 'gy', 'gz'), may hold values from 0 to 1, as said below
- pair_list: int32 [13, 2, 4, 4], P(None, 'gx', 'gy', 'gz'), may hold values 0 or 1
Outputs:
- forces: float32 [3, 2, 4, 4, 1024], P(None, 'gx', 'gy', 'gz')
Inputs may be any that keep to these rules, and one draw needn't show every extreme that they name: `live_mask`: the live slots of each cell are a prefix of its 1024 slots; every cell has at least 256 live slots, and some cell has all 1024 live.
All inputs are finite; a program needn't handle non-finite values. No bound on the sum of `pair_list` on one device may be relied on, other than what follows from the above.
Results may differ from a plain program's by a relative error of at most 0.0003.
Values sent between devices are 32-bit elements; how exact they have to be, the bound alone decides.
A program may use at most 64 MiB of HBM per device.

v0:
```python
import jax
import jax.numpy as jnp
from jax import lax
from jax.sharding import PartitionSpec as P

BLOCK = 128
CORE_WIDTH = 0.1
SPLIT_WIDTH = 2.0
HIGHEST = lax.Precision.HIGHEST
HALF_SHELL = [
    (step_x, step_y, step_z)
    for step_x in (-1, 0, 1)
    for step_y in (-1, 0, 1)
    for step_z in (-1, 0, 1)
    if (step_x, step_y, step_z) > (0, 0, 0)
]


def extended(block, sides, width):
    for axis, dim in sides:
        count = lax.axis_size(axis)
        forward = [(i, i + 1) for i in range(count - 1)]
        forward.append((count - 1, 0))
        backward = [(target, source) for source, target in forward]
        low = lax.ppermute(
            lax.slice_in_dim(block, block.shape[dim] - width, None, axis=dim), axis, forward
        )
        high = lax.ppermute(lax.slice_in_dim(block, 0, width, axis=dim), axis, backward)
        block = jnp.concatenate([low, block, high], axis=dim)
    return block


def from_behind(shard, axis, by):
    size = lax.axis_size(axis)
    return lax.ppermute(shard, axis, [(i, (i + by) % size) for i in range(size)])


def pair_terms(target_mid, target_weight, source_mid, source_weight, offset, with_back):
    coupling = jnp.dot(
        target_weight.T, source_weight, precision=HIGHEST, preferred_element_type=jnp.float32
    )
    deltas = [
        target_mid[component][:, None] - source_mid[component][None, :] - float(offset[component])
        for component in range(3)
    ]
    squared = deltas[0] * deltas[0] + deltas[1] * deltas[1] + deltas[2] * deltas[2]
    inner_inv = lax.rsqrt(squared + CORE_WIDTH * CORE_WIDTH)
    outer_inv = lax.rsqrt(squared + SPLIT_WIDTH * SPLIT_WIDTH)
    strength = coupling * (inner_inv * inner_inv * inner_inv - outer_inv * outer_inv * outer_inv)
    forward = jnp.stack([jnp.sum(strength * delta_part, axis=1) for delta_part in deltas])
    if with_back:
        backward = -jnp.stack([jnp.sum(strength * delta_part, axis=0) for delta_part in deltas])
        return (forward, backward)
    return forward


def line_weights(masked_line, burgers_rows):
    return (burgers_rows[:, None] * masked_line[None]).reshape(9, masked_line.shape[1])


def near_sums(
    target_mid,
    target_weight,
    source_mid,
    source_weight,
    offset,
    target_live,
    source_live,
    with_back,
):
    seg_count = target_mid.shape[1]
    slab = min(4 * BLOCK, seg_count)
    target_slabs = (target_live + slab - 1) // slab
    source_slabs = (source_live + slab - 1) // slab
    empty = jnp.zeros((3, seg_count), jnp.float32)

    def target_step(block_index, carried):
        start = block_index * slab
        part_mid = lax.dynamic_slice_in_dim(target_mid, start, slab, 1)
        part_weight = lax.dynamic_slice_in_dim(target_weight, start, slab, 1)

        def source_step(slab_index, inner):
            anchor = slab_index * slab
            slab_mid = lax.dynamic_slice_in_dim(source_mid, anchor, slab, 1)
            slab_weight = lax.dynamic_slice_in_dim(source_weight, anchor, slab, 1)
            if with_back:
                forward, backward = pair_terms(
                    part_mid, part_weight, slab_mid, slab_weight, offset, True
                )
                previous = lax.dynamic_slice_in_dim(inner[1], anchor, slab, 1)
                return (
                    inner[0] + forward,
                    lax.dynamic_update_slice_in_dim(inner[1], previous + backward, anchor, 1),
                )
            forward = pair_terms(part_mid, part_weight, slab_mid, slab_weight, offset, False)
            return (inner[0] + forward, inner[1])

        block_force, reactions = lax.fori_loop(
            0, source_slabs, source_step, (jnp.zeros((3, slab), jnp.float32), carried[1])
        )
        return (lax.dynamic_update_slice_in_dim(carried[0], block_force, start, 1), reactions)

    return lax.fori_loop(0, target_slabs, target_step, (empty, empty))


def cell_moments(weights, middle, cell_coords):
    offset_rows = [
        middle[component] + (cell_coords[component] % 2).astype(jnp.float32) - 1.0
        for component in range(3)
    ]
    moment_basis = (
        [jnp.ones_like(middle[0])]
        + offset_rows
        + [offset_rows[first] * offset_rows[second] for first in range(3) for second in range(3)]
    )
    return jnp.dot(
        weights, jnp.stack(moment_basis).T, precision=HIGHEST, preferred_element_type=jnp.float32
    )


def far_field(coarse_table, weights, middle, cell_coords, fine_dims, coarse_dims):
    coarse_count = coarse_dims[0] * coarse_dims[1] * coarse_dims[2]
    coarse_index = jnp.arange(coarse_count, dtype=jnp.int32)
    coarse_coords = (
        coarse_index // (coarse_dims[1] * coarse_dims[2]),
        coarse_index // coarse_dims[2] % coarse_dims[1],
        coarse_index % coarse_dims[2],
    )
    displace = []
    for component in range(3):
        cell_gap = cell_coords[component] - 2 * coarse_coords[component]
        cell_gap = (cell_gap + fine_dims[component] // 2) % fine_dims[component] - fine_dims[
            component
        ] // 2
        displace.append(cell_gap.astype(jnp.float32)[:, None] + middle[component][None, :] - 1.0)
    spread = jnp.stack(displace)
    weighted = jnp.einsum(
        "kcq,ci->qki", coarse_table.reshape(coarse_count, 9, 13), weights, precision=HIGHEST
    )
    monopole = weighted[0]
    dipole = weighted[1:4]
    quadrupole = weighted[4:13].reshape(3, 3, coarse_count, weights.shape[1])
    inv_radius = lax.rsqrt(jnp.sum(spread * spread, axis=0) + SPLIT_WIDTH * SPLIT_WIDTH)
    inv_cube = inv_radius * inv_radius * inv_radius
    inv_fifth = inv_cube * inv_radius * inv_radius
    inv_seventh = inv_fifth * inv_radius * inv_radius
    dipole_dot = jnp.sum(dipole * spread, axis=0)
    quad_dot = jnp.sum(quadrupole * spread[None], axis=1)
    quad_form = jnp.sum(spread * quad_dot, axis=0)
    quad_trace = quadrupole[0, 0] + quadrupole[1, 1] + quadrupole[2, 2]
    radial = (
        -monopole * inv_cube
        - 3.0 * dipole_dot * inv_fifth
        - 7.5 * quad_form * inv_seventh
        + 1.5 * quad_trace * inv_fifth
    )
    gradient = spread * radial[None] + dipole * inv_cube[None] + 3.0 * quad_dot * inv_fifth[None]
    return -jnp.sum(gradient, axis=1)


def on_device(midpoints, line_vectors, burgers, live_mask, pair_list):
    seg_count = midpoints.shape[4]
    middle = midpoints.reshape(3, seg_count)
    alive_mask = live_mask.reshape(seg_count).astype(jnp.float32)
    masked_line = line_vectors.reshape(3, seg_count) * alive_mask[None]
    burgers_rows = burgers.reshape(3, seg_count)
    weights = line_weights(masked_line, burgers_rows)
    pair_flags = pair_list.reshape(13).astype(jnp.float32)
    live_count = jnp.sum(live_mask)
    flag_row = jnp.pad(
        jnp.concatenate([pair_flags, live_count.astype(jnp.float32)[None]]), (0, seg_count - 14)
    )
    packed = jnp.concatenate([middle, masked_line, burgers_rows, flag_row[None]], axis=0).reshape(
        10, 1, 1, 1, seg_count
    )
    empty = jnp.zeros((3, seg_count), jnp.float32)
    plane = extended(packed, (("gy", 2), ("gz", 3)), 1)
    upper = from_behind(plane, "gx", -1)
    summed, unused_back = near_sums(
        middle, weights, middle, weights, (0, 0, 0), live_count, live_count, False
    )
    reaction_slots = {}
    for offset_index, offset in enumerate(HALF_SHELL):
        holder = upper if offset[0] == 1 else plane
        source = holder[:, 0, 1 + offset[1], 1 + offset[2]]
        source_weight = line_weights(source[3:6], source[6:9])
        source_live = source[9, 13].astype(jnp.int32)
        forward, backward = lax.cond(
            pair_flags[offset_index] > 0,
            lambda source=source, source_weight=source_weight, source_live=source_live, offset=offset: near_sums(
                middle, weights, source[0:3], source_weight, offset, live_count, source_live, True
            ),
            lambda: (empty, empty),
        )
        summed = summed + forward
        reaction_slots[offset] = backward
    sectioned = jnp.stack(
        [
            jnp.stack(
                [
                    jnp.stack(
                        [
                            reaction_slots.get((step_x, step_y, step_z), empty)
                            for step_z in (-1, 0, 1)
                        ],
                        axis=1,
                    )
                    for step_y in (-1, 0, 1)
                ],
                axis=1,
            )
            for step_x in (-1, 0, 1)
        ],
        axis=1,
    )
    arrived = from_behind(sectioned[:, 2], "gx", 1)
    flat_plane = sectioned[:, 1] + arrived
    plane_up = from_behind(flat_plane[:, 2], "gy", 1)
    plane_down = from_behind(flat_plane[:, 0], "gy", -1)
    column = flat_plane[:, 1] + plane_up + plane_down
    column_up = from_behind(column[:, 2], "gz", 1)
    column_down = from_behind(column[:, 0], "gz", -1)
    summed = summed + column[:, 1] + column_up + column_down
    cell_coords = (lax.axis_index("gx"), lax.axis_index("gy"), lax.axis_index("gz"))
    fine_dims = (lax.axis_size("gx"), lax.axis_size("gy"), lax.axis_size("gz"))
    coarse_dims = (fine_dims[0] // 2, fine_dims[1] // 2, fine_dims[2] // 2)
    coarse_count = coarse_dims[0] * coarse_dims[1] * coarse_dims[2]
    moments = cell_moments(weights, middle, cell_coords).reshape(1, 117)
    coarse_id = (
        cell_coords[0] // 2 * (coarse_dims[1] * coarse_dims[2])
        + cell_coords[1] // 2 * coarse_dims[2]
        + cell_coords[2] // 2
    )
    one_hot = (jnp.arange(coarse_count, dtype=jnp.int32) == coarse_id).astype(jnp.float32)
    coarse_table = lax.psum(one_hot[:, None] * moments, ("gx", "gy", "gz"))
    far = far_field(coarse_table, weights, middle, cell_coords, fine_dims, coarse_dims)
    result = (summed + far) * alive_mask[None]
    return result.reshape(3, 1, 1, 1, seg_count)


def solution(mesh):
    placed = (
        P(None, "gx", "gy", "gz", None),
        P(None, "gx", "gy", "gz", None),
        P(None, "gx", "gy", "gz", None),
        P("gx", "gy", "gz", None),
        P(None, "gx", "gy", "gz"),
    )
    return jax.shard_map(
        on_device,
        mesh=mesh,
        in_specs=placed,
        out_specs=P(None, "gx", "gy", "gz", None),
        check_vma=False,
    )
```

profile of v0, /device:TPU:1, one launch (start us, length us, event | category | flops | bytes accessed | tf_op | source)
XLA Modules:
  0.0 265.5 jit_solution(8251189360535266189)
XLA Ops:
  3.7 2.6 collective-permute-start
  7.7 7.9 %while.599 = (s32[]{:T(128)}, f32[3,1024]{1,0:T(4,128)S(1)}, s32[]{:T(128)}, f32[9,1024]{1,0:T(8,128)S(1)}, f32[3,1024]{1,0:T(4,128)S(1)}, /*index=5*/s32[]{:T(1...) while((s32[]{:T(128)}, f32[3,1024]{1,0:T(4,128)S(1)}, ...), condition=%wide.region_7.8_spmd, body=%wide.region_1.7_spmd.sunk | while | flops 34081804 | bytes 199190 | solution.py:103
  7.8 3.8 %while.600 = (s32[]{:T(128)}, f32[3,512]{1,0:T(4,128)S(1)}, s32[]{:T(128)}, f32[9,1024]{1,0:T(8,128)S(1)}, f32[9,512]{1,0:T(8,128)S(1)}, /*index=5*/f32[3,512]{1...) while((s32[]{:T(128)}, f32[3,512]{1,0:T(4,128)S(1)}, ...), condition=%wide.region_6.6_spmd, body=%wide.region_2.5_spmd.sunk | while | flops 34081800 | bytes 127187 | solution.py:98
  11.7 3.8 %while.600 = (s32[]{:T(128)}, f32[3,512]{1,0:T(4,128)S(1)}, s32[]{:T(128)}, f32[9,1024]{1,0:T(8,128)S(1)}, f32[9,512]{1,0:T(8,128)S(1)}, /*index=5*/f32[3,512]{1...) while((s32[]{:T(128)}, f32[3,512]{1,0:T(4,128)S(1)}, ...), condition=%wide.region_6.6_spmd, body=%wide.region_2.5_spmd.sunk | while | flops 34081800 | bytes 127187 | solution.py:98
  16.3 38.6 %psum.7 = f32[4,9,13]{1,2,0:T(8,128)S(1)} all-reduce(f32[4,9,13]{1,2,0:T(8,128)S(1)} %copy.56), channel_id=1, replica_groups=mesh['gx'=2,'gy'=4,'gz'=4] {'gx','gy','gz'}, use_global_device_ids=true, to_apply=%region_164.165 | all-reduce | flops 468 | bytes 3744 | tf_op jit(solution)/shard_map/psum | solution.py:235
  56.7 2.0 collective-permute-start.2
  59.0 2.1 collective-permute-done.3
  61.1 2.0 collective-permute-done.2
  76.1 11.2 %conditional.16 = (f32[3,1024]{1,0:T(4,128)}, f32[3,1,1024]{2,0,1:T(4,128)}) conditional(s32[]{:T(128)} %bitcast.265, () %tuple.632, (s32[]{:T(128)}, f32[10,1,3,1,1024]{4,1,3,2,0:T(1,128)S(1)}, f32[9,1024]{1,0:T(8,128)S(1)}, f32[3,1024]{1,0:T(4,128)S(1)}) %tuple.1456), branch_computations={%region_44.45_spmd, %region_45.56_spmd} | conditional | flops 35406380 | bytes 787566 | solution.py:188
  79.3 8.0 %while.570 = (s32[]{:T(128)}, f32[3,1024]{1,0:T(4,128)}, f32[3,1024]{1,0:T(4,128)}, s32[]{:T(128)}, f32[9,1024]{1,0:T(8,128)S(1)}, /*index=5*/f32[3,1024]{1,0:T(...) while((s32[]{:T(128)}, f32[3,1024]{1,0:T(4,128)}, ...), condition=%wide.region_55.55_spmd.clone, body=%wide.region_46.54_spmd.clone.sunk | while | flops 35406348 | bytes 361042 | solution.py:103
  79.4 3.3 %while.610 = (s32[]{:T(128)}, f32[3,512]{1,0:T(4,128)S(1)}, f32[3,1024]{1,0:T(4,128)}, s32[]{:T(128)}, f32[9,1024]{1,0:T(8,128)S(1)}, /*index=5*/f32[9,512]{1,0:...) while((s32[]{:T(128)}, f32[3,512]{1,0:T(4,128)S(1)}, ...), condition=%wide.region_54.53_spmd, body=%wide.region_47.52_spmd.sunk | while | flops 35397128 | bytes 155871 | solution.py:98
  83.4 3.3 %while.610 = (s32[]{:T(128)}, f32[3,512]{1,0:T(4,128)S(1)}, f32[3,1024]{1,0:T(4,128)}, s32[]{:T(128)}, f32[9,1024]{1,0:T(8,128)S(1)}, /*index=5*/f32[9,512]{1,0:...) while((s32[]{:T(128)}, f32[3,512]{1,0:T(4,128)S(1)}, ...), condition=%wide.region_54.53_spmd, body=%wide.region_47.52_spmd.sunk | while | flops 35397128 | bytes 155871 | solution.py:98
  87.3 8.1 %conditional.13 = (f32[3,1024]{1,0:T(4,128)}, f32[3,1,3,1024]{3,0,2,1:T(4,128)S(1)}) conditional(s32[]{:T(128)} %bitcast.259, () %tuple.626, (s32[]{:T(128)}, f32[10,1,3,1,1024]{4,1,3,2,0:T(1,128)S(1)}, f32[9,1024]{1,0:T(8,128)S(1)}, f32[3,1024]{1,0:T(4,128)S(1)}) %tuple.1457), branch_computations={%region_8.9_spmd, %region_9.20_spmd} | conditional | flops 35144236 | bytes 840814 | solution.py:188
  90.0 5.4 %while.561 = (s32[]{:T(128)}, f32[3,1024]{1,0:T(4,128)}, f32[3,1024]{1,0:T(4,128)S(1)}, s32[]{:T(128)}, f32[9,1024]{1,0:T(8,128)S(1)}, /*index=5*/f32[3,1024]{1,...) while((s32[]{:T(128)}, f32[3,1024]{1,0:T(4,128)}, ...), condition=%wide.region_19.19_spmd.clone, body=%wide.region_10.18_spmd.clone.sunk | while | flops 35144204 | bytes 365138 | solution.py:103
  90.0 2.0 while.613
  92.8 2.0 while.613
  96.1 17.7 %conditional.14 = (f32[3,1024]{1,0:T(4,128)}, f32[3,1,1024]{2,0,1:T(4,128)}) conditional(s32[]{:T(128)} %bitcast.263, () %tuple.628, (s32[]{:T(128)}, f32[10,1,3,1,1024]{4,1,3,2,0:T(1,128)S(1)}, f32[9,1024]{1,0:T(8,128)S(1)}, f32[3,1024]{1,0:T(4,128)S(1)}) %tuple.1468), branch_computations={%region_20.21_spmd, %region_21.32_spmd} | conditional | flops 35406380 | bytes 787566 | solution.py:188
  99.2 14.6 %while.564 = (s32[]{:T(128)}, f32[3,1024]{1,0:T(4,128)}, f32[3,1024]{1,0:T(4,128)}, s32[]{:T(128)}, f32[9,1024]{1,0:T(8,128)S(1)}, /*index=5*/f32[3,1024]{1,0:T(...) while((s32[]{:T(128)}, f32[3,1024]{1,0:T(4,128)}, ...), condition=%wide.region_31.31_spmd.clone, body=%wide.region_22.30_spmd.clone.sunk | while | flops 35406348 | bytes 361042 | solution.py:103
  99.2 6.7 %while.612 = (s32[]{:T(128)}, f32[3,512]{1,0:T(4,128)S(1)}, f32[3,1024]{1,0:T(4,128)}, s32[]{:T(128)}, f32[9,1024]{1,0:T(8,128)S(1)}, /*index=5*/f32[9,512]{1,0:...) while((s32[]{:T(128)}, f32[3,512]{1,0:T(4,128)S(1)}, ...), condition=%wide.region_30.29_spmd, body=%wide.region_23.28_spmd.sunk | while | flops 35397128 | bytes 155871 | solution.py:98
  106.5 6.6 %while.612 = (s32[]{:T(128)}, f32[3,512]{1,0:T(4,128)S(1)}, f32[3,1024]{1,0:T(4,128)}, s32[]{:T(128)}, f32[9,1024]{1,0:T(8,128)S(1)}, /*index=5*/f32[9,512]{1,0:...) while((s32[]{:T(128)}, f32[3,512]{1,0:T(4,128)S(1)}, ...), condition=%wide.region_30.29_spmd, body=%wide.region_23.28_spmd.sunk | while | flops 35397128 | bytes 155871 | solution.py:98
  113.8 19.0 %conditional.25 = (f32[3,1024]{1,0:T(4,128)}, f32[3,1,1024]{2,0,1:T(4,128)}) conditional(s32[]{:T(128)} %bitcast.274, () %tuple.642, (s32[]{:T(128)}, f32[10,1,3,3,1024]{4,1,3,2,0:T(1,128)}, f32[9,1024]{1,0:T(8,128)S(1)}, f32[3,1024]{1,0:T(4,128)S(1)}) %tuple.1459), branch_computations={%region_152.153_spmd, %region_153.164_spmd} | conditional | flops 35668524 | bytes 1279086 | solution.py:188
  117.9 14.8 %while.597 = (s32[]{:T(128)}, f32[3,1024]{1,0:T(4,128)}, f32[3,1024]{1,0:T(4,128)}, s32[]{:T(128)}, f32[9,1024]{1,0:T(8,128)S(1)}, /*index=5*/f32[3,1024]{1,0:T(...) while((s32[]{:T(128)}, f32[3,1024]{1,0:T(4,128)}, ...), condition=%wide.region_163.163_spmd.clone, body=%wide.region_154.162_spmd.clone.sunk | while | flops 35668492 | bytes 361042 | solution.py:103
  118.0 6.7 %while.601 = (s32[]{:T(128)}, f32[3,512]{1,0:T(4,128)S(1)}, f32[3,1024]{1,0:T(4,128)}, s32[]{:T(128)}, f32[9,1024]{1,0:T(8,128)S(1)}, /*index=5*/f32[9,512]{1,0:...) while((s32[]{:T(128)}, f32[3,512]{1,0:T(4,128)S(1)}, ...), condition=%wide.region_162.161_spmd, body=%wide.region_155.160_spmd.sunk | while | flops 35659272 | bytes 155871 | solution.py:98
  125.4 6.7 %while.601 = (s32[]{:T(128)}, f32[3,512]{1,0:T(4,128)S(1)}, f32[3,1024]{1,0:T(4,128)}, s32[]{:T(128)}, f32[9,1024]{1,0:T(8,128)S(1)}, /*index=5*/f32[9,512]{1,0:...) while((s32[]{:T(128)}, f32[3,512]{1,0:T(4,128)S(1)}, ...), condition=%wide.region_162.161_spmd, body=%wide.region_155.160_spmd.sunk | while | flops 35659272 | bytes 155871 | solution.py:98
  132.7 18.7 %conditional.24 = (f32[3,1024]{1,0:T(4,128)}, f32[3,1,1024]{2,0,1:T(4,128)}) conditional(s32[]{:T(128)} %bitcast.273, () %tuple.641, (s32[]{:T(128)}, f32[10,1,3,3,1024]{4,1,3,2,0:T(1,128)}, f32[9,1024]{1,0:T(8,128)S(1)}, f32[3,1024]{1,0:T(4,128)S(1)}) %tuple.1460), branch_computations={%region_140.141_spmd, %region_141.152_spmd} | conditional | flops 35406380 | bytes 1279086 | solution.py:188
  136.9 14.6 %while.594 = (s32[]{:T(128)}, f32[3,1024]{1,0:T(4,128)}, f32[3,1024]{1,0:T(4,128)}, s32[]{:T(128)}, f32[9,1024]{1,0:T(8,128)S(1)}, /*index=5*/f32[3,1024]{1,0:T(...) while((s32[]{:T(128)}, f32[3,1024]{1,0:T(4,128)}, ...), condition=%wide.region_151.151_spmd.clone, body=%wide.region_142.150_spmd.clone.sunk | while | flops 35406348 | bytes 361042 | solution.py:103
  136.9 6.6 %while.602 = (s32[]{:T(128)}, f32[3,512]{1,0:T(4,128)S(1)}, f32[3,1024]{1,0:T(4,128)}, s32[]{:T(128)}, f32[9,1024]{1,0:T(8,128)S(1)}, /*index=5*/f32[9,512]{1,0:...) while((s32[]{:T(128)}, f32[3,512]{1,0:T(4,128)S(1)}, ...), condition=%wide.region_150.149_spmd, body=%wide.region_143.148_spmd.sunk | while | flops 35397128 | bytes 155871 | solution.py:98
  144.2 6.6 %while.602 = (s32[]{:T(128)}, f32[3,512]{1,0:T(4,128)S(1)}, f32[3,1024]{1,0:T(4,128)}, s32[]{:T(128)}, f32[9,1024]{1,0:T(8,128)S(1)}, /*index=5*/f32[9,512]{1,0:...) while((s32[]{:T(128)}, f32[3,512]{1,0:T(4,128)S(1)}, ...), condition=%wide.region_150.149_spmd, body=%wide.region_143.148_spmd.sunk | while | flops 35397128 | bytes 155871 | solution.py:98
  155.1 18.8 %conditional.20 = (f32[3,1024]{1,0:T(4,128)}, f32[3,1,1024]{2,0,1:T(4,128)}) conditional(s32[]{:T(128)} %bitcast.269, () %tuple.637, (s32[]{:T(128)}, f32[10,1,3,3,1024]{4,1,3,2,0:T(1,128)}, f32[9,1024]{1,0:T(8,128)S(1)}, f32[3,1024]{1,0:T(4,128)S(1)}) %tuple.1464), branch_computations={%region_92.93_spmd, %region_93.104_spmd} | conditional | flops 35406380 | bytes 1279086 | solution.py:188
  159.2 14.6 %while.582 = (s32[]{:T(128)}, f32[3,1024]{1,0:T(4,128)}, f32[3,1024]{1,0:T(4,128)}, s32[]{:T(128)}, f32[9,1024]{1,0:T(8,128)S(1)}, /*index=5*/f32[3,1024]{1,0:T(...) while((s32[]{:T(128)}, f32[3,1024]{1,0:T(4,128)}, ...), condition=%wide.region_103.103_spmd.clone, body=%wide.region_94.102_spmd.clone.sunk | while | flops 35406348 | bytes 361042 | solution.py:103
  159.3 6.7 %while.606 = (s32[]{:T(128)}, f32[3,512]{1,0:T(4,128)S(1)}, f32[3,1024]{1,0:T(4,128)}, s32[]{:T(128)}, f32[9,1024]{1,0:T(8,128)S(1)}, /*index=5*/f32[9,512]{1,0:...) while((s32[]{:T(128)}, f32[3,512]{1,0:T(4,128)S(1)}, ...), condition=%wide.region_102.101_spmd, body=%wide.region_95.100_spmd.sunk | while | flops 35397128 | bytes 155871 | solution.py:98
  166.6 6.7 %while.606 = (s32[]{:T(128)}, f32[3,512]{1,0:T(4,128)S(1)}, f32[3,1024]{1,0:T(4,128)}, s32[]{:T(128)}, f32[9,1024]{1,0:T(8,128)S(1)}, /*index=5*/f32[9,512]{1,0:...) while((s32[]{:T(128)}, f32[3,512]{1,0:T(4,128)S(1)}, ...), condition=%wide.region_102.101_spmd, body=%wide.region_95.100_spmd.sunk | while | flops 35397128 | bytes 155871 | solution.py:98
  173.9 12.2 %conditional.19 = (f32[3,1024]{1,0:T(4,128)}, f32[3,1,1024]{2,0,1:T(4,128)}) conditional(s32[]{:T(128)} %bitcast.268, () %tuple.636, (s32[]{:T(128)}, f32[10,1,3,3,1024]{4,1,3,2,0:T(1,128)}, f32[9,1024]{1,0:T(8,128)S(1)}, f32[3,1024]{1,0:T(4,128)S(1)}) %tuple.1465), branch_computations={%region_80.81_spmd, %region_81.92_spmd} | conditional | flops 35668524 | bytes 1279086 | solution.py:188
  178.0 8.1 %while.579 = (s32[]{:T(128)}, f32[3,1024]{1,0:T(4,128)}, f32[3,1024]{1,0:T(4,128)}, s32[]{:T(128)}, f32[9,1024]{1,0:T(8,128)S(1)}, /*index=5*/f32[3,1024]{1,0:T(...) while((s32[]{:T(128)}, f32[3,1024]{1,0:T(4,128)}, ...), condition=%wide.region_91.91_spmd.clone, body=%wide.region_82.90_spmd.clone.sunk | while | flops 35668492 | bytes 361042 | solution.py:103
  178.1 3.4 %while.607 = (s32[]{:T(128)}, f32[3,512]{1,0:T(4,128)S(1)}, f32[3,1024]{1,0:T(4,128)}, s32[]{:T(128)}, f32[9,1024]{1,0:T(8,128)S(1)}, /*index=5*/f32[9,512]{1,0:...) while((s32[]{:T(128)}, f32[3,512]{1,0:T(4,128)S(1)}, ...), condition=%wide.region_90.89_spmd, body=%wide.region_83.88_spmd.sunk | while | flops 35659272 | bytes 155871 | solution.py:98
  182.1 3.4 %while.607 = (s32[]{:T(128)}, f32[3,512]{1,0:T(4,128)S(1)}, f32[3,1024]{1,0:T(4,128)}, s32[]{:T(128)}, f32[9,1024]{1,0:T(8,128)S(1)}, /*index=5*/f32[9,512]{1,0:...) while((s32[]{:T(128)}, f32[3,512]{1,0:T(4,128)S(1)}, ...), condition=%wide.region_90.89_spmd, body=%wide.region_83.88_spmd.sunk | while | flops 35659272 | bytes 155871 | solution.py:98
  186.1 18.7 %conditional.18 = (f32[3,1024]{1,0:T(4,128)}, f32[3,1,1024]{2,0,1:T(4,128)}) conditional(s32[]{:T(128)} %bitcast.267, () %tuple.635, (s32[]{:T(128)}, f32[10,1,3,3,1024]{4,1,3,2,0:T(1,128)}, f32[9,1024]{1,0:T(8,128)S(1)}, f32[3,1024]{1,0:T(4,128)S(1)}) %tuple.1466), branch_computations={%region_68.69_spmd, %region_69.80_spmd} | conditional | flops 35406380 | bytes 1279086 | solution.py:188
  190.2 14.6 %while.576 = (s32[]{:T(128)}, f32[3,1024]{1,0:T(4,128)}, f32[3,1024]{1,0:T(4,128)}, s32[]{:T(128)}, f32[9,1024]{1,0:T(8,128)S(1)}, /*index=5*/f32[3,1024]{1,0:T(...) while((s32[]{:T(128)}, f32[3,1024]{1,0:T(4,128)}, ...), condition=%wide.region_79.79_spmd.clone, body=%wide.region_70.78_spmd.clone.sunk | while | flops 35406348 | bytes 361042 | solution.py:103
  190.3 6.6 %while.608 = (s32[]{:T(128)}, f32[3,512]{1,0:T(4,128)S(1)}, f32[3,1024]{1,0:T(4,128)}, s32[]{:T(128)}, f32[9,1024]{1,0:T(8,128)S(1)}, /*index=5*/f32[9,512]{1,0:...) while((s32[]{:T(128)}, f32[3,512]{1,0:T(4,128)S(1)}, ...), condition=%wide.region_78.77_spmd, body=%wide.region_71.76_spmd.sunk | while | flops 35397128 | bytes 155871 | solution.py:98
  197.6 6.6 %while.608 = (s32[]{:T(128)}, f32[3,512]{1,0:T(4,128)S(1)}, f32[3,1024]{1,0:T(4,128)}, s32[]{:T(128)}, f32[9,1024]{1,0:T(8,128)S(1)}, /*index=5*/f32[9,512]{1,0:...) while((s32[]{:T(128)}, f32[3,512]{1,0:T(4,128)S(1)}, ...), condition=%wide.region_78.77_spmd, body=%wide.region_71.76_spmd.sunk | while | flops 35397128 | bytes 155871 | solution.py:98
  204.8 12.3 %conditional.17 = (f32[3,1024]{1,0:T(4,128)}, f32[3,1,1024]{2,0,1:T(4,128)}) conditional(s32[]{:T(128)} %bitcast.266, () %tuple.633, (s32[]{:T(128)}, f32[10,1,3,3,1024]{4,1,3,2,0:T(1,128)}, f32[9,1024]{1,0:T(8,128)S(1)}, f32[3,1024]{1,0:T(4,128)S(1)}) %tuple.1467), branch_computations={%region_56.57_spmd, %region_57.68_spmd} | conditional | flops 35668524 | bytes 1279086 | solution.py:188
  209.0 8.1 %while.573 = (s32[]{:T(128)}, f32[3,1024]{1,0:T(4,128)}, f32[3,1024]{1,0:T(4,128)}, s32[]{:T(128)}, f32[9,1024]{1,0:T(8,128)S(1)}, /*index=5*/f32[3,1024]{1,0:T(...) while((s32[]{:T(128)}, f32[3,1024]{1,0:T(4,128)}, ...), condition=%wide.region_67.67_spmd.clone, body=%wide.region_58.66_spmd.clone.sunk | while | flops 35668492 | bytes 361042 | solution.py:103
  209.1 3.4 %while.609 = (s32[]{:T(128)}, f32[3,512]{1,0:T(4,128)S(1)}, f32[3,1024]{1,0:T(4,128)}, s32[]{:T(128)}, f32[9,1024]{1,0:T(8,128)S(1)}, /*index=5*/f32[9,512]{1,0:...) while((s32[]{:T(128)}, f32[3,512]{1,0:T(4,128)S(1)}, ...), condition=%wide.region_66.65_spmd, body=%wide.region_59.64_spmd.sunk | while | flops 35659272 | bytes 155871 | solution.py:98
  213.1 3.4 %while.609 = (s32[]{:T(128)}, f32[3,512]{1,0:T(4,128)S(1)}, f32[3,1024]{1,0:T(4,128)}, s32[]{:T(128)}, f32[9,1024]{1,0:T(8,128)S(1)}, /*index=5*/f32[9,512]{1,0:...) while((s32[]{:T(128)}, f32[3,512]{1,0:T(4,128)S(1)}, ...), condition=%wide.region_66.65_spmd, body=%wide.region_59.64_spmd.sunk | while | flops 35659272 | bytes 155871 | solution.py:98
  220.3 3.2 %collective-permute-done.5 = f32[3,3,3,1024]{3,0,2,1:T(4,128)S(1)} collective-permute-done((f32[3,3,3,1024]{3,0,2,1:T(4,128)S(1)}, f32[3,3,3,1024]{3,0,2,1:T(4,128)S(1)}, u32[]{:S(2)}, u32[]{:S(2)}) %collective-permute-start.5) | collective-permute-done | bytes 110624 | tf_op jit(solution)/shard_map/ppermute | solution.py:35
  225.0 2.3 collective-permute-done.7
  227.4 3.3 %collective-permute-start.9 = (f32[3,1024]{1,0:T(4,128)S(1)}, f32[3,1024]{1,0:T(4,128)S(1)}, u32[]{:S(2)}, u32[]{:S(2)}) collective-permute-start(f32[3,1024]{1,0:T(4,128)S(1)} %get-tuple-element.5495), channel_id=1, source_target_pairs={{0,3},{1,0},{2,1},{3,2},{4,7},{5,4},{6,5},{7,6},{8,11},{9,8},{10,9... | collective-permute-start | bytes 36872 | tf_op jit(solution)/shard_map/ppermute | solution.py:35
  231.8 31.5 %collective-permute-done.9 = f32[3,1024]{1,0:T(4,128)S(1)} collective-permute-done((f32[3,1024]{1,0:T(4,128)S(1)}, f32[3,1024]{1,0:T(4,128)S(1)}, u32[]{:S(2)}, u32[]{:S(2)}) %collective-permute-start.9) | collective-permute-done | bytes 12320 | tf_op jit(solution)/shard_map/ppermute | solution.py:35
  (421 shorter events, 159.8 us)
Async XLA Ops:
  0.7 2.2 copy-start.22
  2.1 0.7 copy-start.19
  2.8 0.7 copy-start.15
  2.8 0.7 copy-start.21
  3.6 51.8 %collective-permute-start.1 = (f32[10,1,1,1,1024]{4,1,3,2,0:T(1,128)S(1)}, f32[10,1,1,1,1024]{4,1,3,2,0:T(1,128)S(1)}, u32[]{:S(2)}, u32[]{:S(2)}) collective-permute-start(f32[10,1,1,1,1024]{4,1,3,2,0:T(1,128)S(1)} %reshape.936), channel_id=1, source_target_pairs={{4,0},{8,4},{12,8},{0,12},{5,1},{9,5},{13,9},{1,13},{6,2},{10,6},{... | collective-permute-start | bytes 122888 | tf_op jit(solution)/shard_map/ppermute | solution.py:28
  3.7 51.7 %collective-permute-start = (f32[10,1,1,1,1024]{4,1,3,2,0:T(1,128)S(1)}, f32[10,1,1,1,1024]{4,1,3,2,0:T(1,128)S(1)}, u32[]{:S(2)}, u32[]{:S(2)}) collective-permute-start(f32[10,1,1,1,1024]{4,1,3,2,0:T(1,128)S(1)} %reshape.936), channel_id=1, source_target_pairs={{0,4},{4,8},{8,12},{12,0},{1,5},{5,9},{9,13},{13,1},{2,6},{6,10},{... | collective-permute-start | bytes 122888 | tf_op jit(solution)/shard_map/ppermute | solution.py:25
  15.6 0.6 copy-start.16
  55.3 18.9 %copy-start.7 = (f32[1,4,1024]{2,1,0:T(4,128)}, f32[1,4,1024]{2,1,0:T(4,128)S(1)}, u32[]{:S(2)}) copy-start(f32[1,4,1024]{2,1,0:T(4,128)S(1)} %get-tuple-element.5525) | copy-start | bytes 49156
  55.3 18.9 %copy-start.9 = (f32[1,4,1024]{2,1,0:T(4,128)}, f32[1,4,1024]{2,1,0:T(4,128)S(1)}, u32[]{:S(2)}) copy-start(f32[1,4,1024]{2,1,0:T(4,128)S(1)} %get-tuple-element.5526) | copy-start | bytes 49156
  55.4 18.8 %copy-start.5 = (f32[1,4,1024]{2,1,0:T(4,128)}, f32[1,4,1024]{2,1,0:T(4,128)S(1)}, u32[]{:S(2)}) copy-start(f32[1,4,1024]{2,1,0:T(4,128)S(1)} %add_add_fusion.2) | copy-start | bytes 49156
  55.5 5.7 %collective-permute-start.3 = (f32[10,1,3,1,1024]{4,1,3,2,0:T(1,128)S(1)}, f32[10,1,3,1,1024]{4,1,3,2,0:T(1,128)S(1)}, u32[]{:S(2)}, u32[]{:S(2)}) collective-permute-start(f32[10,1,3,1,1024]{4,1,3,2,0:T(1,128)S(1)} %constant_dynamic-update-slice_fusion.14), channel_id=1, source_target_pairs={{0,1},{1,2},{2,3},{3,0},{4,5},{5,6},{6,7},{7,4},{8,9},{9,10},{10,1... | collective-permute-start | bytes 368648 | tf_op jit(solution)/shard_map/ppermute | solution.py:25
  56.7 6.4 %collective-permute-start.2 = (f32[10,1,3,1,1024]{4,1,3,2,0:T(1,128)S(1)}, f32[10,1,3,1,1024]{4,1,3,2,0:T(1,128)S(1)}, u32[]{:S(2)}, u32[]{:S(2)}) collective-permute-start(f32[10,1,3,1,1024]{4,1,3,2,0:T(1,128)S(1)} %constant_dynamic-update-slice_fusion.14), channel_id=1, source_target_pairs={{1,0},{2,1},{3,2},{0,3},{5,4},{6,5},{7,6},{4,7},{9,8},{10,9},{11,1... | collective-permute-start | bytes 368648 | tf_op jit(solution)/shard_map/ppermute | solution.py:28
  58.9 15.3 %copy-start = (f32[1024,4,13]{0,1,2:T(4,128)}, f32[1024,4,13]{0,1,2:T(4,128)S(1)}, u32[]{:S(2)}) copy-start(f32[1024,4,13]{0,1,2:T(4,128)S(1)} %copy.69) | copy-start | bytes 638980
  59.0 15.2 %copy-start.3 = (f32[3,4,1024]{2,1,0:T(4,128)}, f32[3,4,1024]{2,1,0:T(4,128)S(1)}, u32[]{:S(2)}) copy-start(f32[3,4,1024]{2,1,0:T(4,128)S(1)} %multiply_reduce_fusion) | copy-start | bytes 147460
  61.1 3.1 %copy-start.1 = (f32[10,1,3,1,1024]{4,1,3,2,0:T(1,128)}, f32[10,1,3,1,1024]{4,1,3,2,0:T(1,128)S(1)}, u32[]{:S(2)}) copy-start(f32[10,1,3,1,1024]{4,1,3,2,0:T(1,128)S(1)} %collective-permute-done.3) | copy-start | bytes 368644
  64.2 49.6 %collective-permute-start.4 = (f32[10,1,3,3,1024]{4,1,3,2,0:T(1,128)}, f32[10,1,3,3,1024]{4,1,3,2,0:T(1,128)}, u32[]{:S(2)}, u32[]{:S(2)}) collective-permute-start(f32[10,1,3,3,1024]{4,1,3,2,0:T(1,128)} %pad_maximum_fusion), channel_id=1, source_target_pairs={{0,16},{16,0},{1,17},{17,1},{2,18},{18,2},{3,19},{19,3},{4,20},{20... | collective-permute-start | bytes 1105928 | tf_op jit(solution)/shard_map/ppermute | solution.py:35
  74.2 0.7 copy-start.13
  87.3 8.1 %copy-start.2 = (f32[10,1,3,1,1024]{4,1,3,2,0:T(1,128)S(1)}, f32[10,1,3,1,1024]{4,1,3,2,0:T(1,128)}, u32[]{:S(2)}) copy-start(f32[10,1,3,1,1024]{4,1,3,2,0:T(1,128)} %copy-done.1) | copy-start | bytes 368644
  95.4 0.6 copy-start.11
  219.5 4.1 %collective-permute-start.5 = (f32[3,3,3,1024]{3,0,2,1:T(4,128)S(1)}, f32[3,3,3,1024]{3,0,2,1:T(4,128)S(1)}, u32[]{:S(2)}, u32[]{:S(2)}) collective-permute-start(f32[3,3,3,1024]{3,0,2,1:T(4,128)S(1)} %pad_maximum_fusion.1), channel_id=1, source_target_pairs={{0,16},{16,0},{1,17},{17,1},{2,18},{18,2},{3,19},{19,3},{4,20},{20... | collective-permute-start | bytes 331784 | tf_op jit(solution)/shard_map/ppermute | solution.py:35
  219.6 4.0 %copy-start.12 = (f32[3,1,3,1024]{3,0,2,1:T(4,128)S(1)}, f32[3,1,3,1024]{3,0,2,1:T(4,128)}, u32[]{:S(2)}) copy-start(f32[3,1,3,1024]{3,0,2,1:T(4,128)} %copy-done.11) | copy-start | bytes 110596
  220.3 3.2 %copy-start.23 = (f32[3]{0:T(128)S(1)}, f32[3]{0:T(128)}, u32[]{:S(2)}) copy-start(f32[3]{0:T(128)} %pad.105.clone) | copy-start | bytes 40
  223.6 0.7 copy-start.14
  223.7 1.3 collective-permute-start.6
  223.7 3.6 %collective-permute-start.7 = (f32[3,3,1024]{2,0,1:T(4,128)S(1)}, f32[3,3,1024]{2,0,1:T(4,128)S(1)}, u32[]{:S(2)}, u32[]{:S(2)}) collective-permute-start(f32[3,3,1024]{2,0,1:T(4,128)S(1)} %get-tuple-element.5493), channel_id=1, source_target_pairs={{0,12},{4,0},{8,4},{12,8},{1,13},{5,1},{9,5},{13,9},{2,14},{6,2},{... | collective-permute-start | bytes 110600 | tf_op jit(solution)/shard_map/ppermute | solution.py:35
  227.3 3.4 %copy-start.8 = (f32[1,4,1024]{2,1,0:T(4,128)S(1)}, f32[1,4,1024]{2,1,0:T(4,128)}, u32[]{:S(2)}) copy-start(f32[1,4,1024]{2,1,0:T(4,128)} %copy-done.7) | copy-start | bytes 49156
  227.3 3.4 %copy-start.10 = (f32[1,4,1024]{2,1,0:T(4,128)S(1)}, f32[1,4,1024]{2,1,0:T(4,128)}, u32[]{:S(2)}) copy-start(f32[1,4,1024]{2,1,0:T(4,128)} %copy-done.9) | copy-start | bytes 49156
  227.3 3.4 %copy-start.18 = (f32[4,1024]{1,0:T(4,128)S(1)}, f32[4,1024]{1,0:T(4,128)}, u32[]{:S(2)}) copy-start(f32[4,1024]{1,0:T(4,128)} %fusion.244) | copy-start | bytes 49156
  227.3 3.4 %copy-start.4 = (f32[3,4,1024]{2,1,0:T(4,128)S(1)}, f32[3,4,1024]{2,1,0:T(4,128)}, u32[]{:S(2)}) copy-start(f32[3,4,1024]{2,1,0:T(4,128)} %copy-done.3) | copy-start | bytes 147460
  227.3 3.4 %copy-start.6 = (f32[1,4,1024]{2,1,0:T(4,128)S(1)}, f32[1,4,1024]{2,1,0:T(4,128)}, u32[]{:S(2)}) copy-start(f32[1,4,1024]{2,1,0:T(4,128)} %copy-done.5) | copy-start | bytes 49156
  227.4 4.4 %collective-permute-start.8 = (f32[3,1024]{1,0:T(4,128)S(1)}, f32[3,1024]{1,0:T(4,128)S(1)}, u32[]{:S(2)}, u32[]{:S(2)}) collective-permute-start(f32[3,1024]{1,0:T(4,128)S(1)} %get-tuple-element.5494), channel_id=1, source_target_pairs={{0,1},{1,2},{2,3},{3,0},{4,5},{5,6},{6,7},{7,4},{8,9},{9,10},{10,1... | collective-permute-start | bytes 36872 | tf_op jit(solution)/shard_map/ppermute | solution.py:35
  227.4 35.8 %collective-permute-start.9 = (f32[3,1024]{1,0:T(4,128)S(1)}, f32[3,1024]{1,0:T(4,128)S(1)}, u32[]{:S(2)}, u32[]{:S(2)}) collective-permute-start(f32[3,1024]{1,0:T(4,128)S(1)} %get-tuple-element.5495), channel_id=1, source_target_pairs={{0,3},{1,0},{2,1},{3,2},{4,7},{5,4},{6,5},{7,6},{8,11},{9,8},{10,9... | collective-permute-start | bytes 36872 | tf_op jit(solution)/shard_map/ppermute | solution.py:35
  231.6 31.7 %copy-start.17 = (f32[3,1024]{1,0:T(4,128)S(1)}, f32[3,1024]{1,0:T(4,128)}, u32[]{:S(2)}) copy-start(f32[3,1024]{1,0:T(4,128)} %copy-done.16) | copy-start | bytes 36868
  263.3 0.7 copy-start.20
where the time goes:
time: 269 us; the launch traced here: 266 us
  matrix products  61.3 us (23%)
  local copies, waits for them, and re-layouts  46.4 us (17%)
  other arithmetic  44 us (16%)
  waiting for transfers between devices  42 us (16%)
  blocking collectives  38.6 us (14%)
  loops' own time  12.8 us (5%)
  starting transfers between devices  10.5 us (4%)
  between operations  9.99 us (4%)
    dot_general x32, matrix products, pair_terms(): jnp.dot(target_weight.T, source_weight, precision=HIGHEST, preferred_elem...  60.7 us
    psum x1, blocking collectives, on_device(): coarse_table = lax.psum(one_hot[:, None] * moments, ('gx', 'gy', 'gz'))  38.6 us
    ppermute x6, waiting for transfers between devices, from_behind(): lax.ppermute(shard, axis, [(i, (i + by) % size) for i in range(size)])  37.8 us
    add x28, other arithmetic, source_step(): inner[0] + forward  34.3 us
    another operation x52, local copies, waits for them, and re-layouts  19.3 us
    another operation x13, loops' own time, on_device(): lax.cond(pair_flags[offset_index] > 0, lambda source=source, source_weigh...  11.6 us
    dynamic_update_slice x20, local copies, waits for them, and re-layouts, target_step(): lax.dynamic_update_slice_in_dim(carried[0], block_force, start, 1)  10.8 us
  transfers between devices with their start and end apart: 10, of which 7 were waited for; matrix products, arithmetic and copies ran while one was open for 18% of the time, Pallas kernels for 0%

commit v1 on v0

--- a/solution.py
+++ b/solution.py
@@ -232,7 +232,9 @@
         + cell_coords[2] // 2
     )
     one_hot = (jnp.arange(coarse_count, dtype=jnp.int32) == coarse_id).astype(jnp.float32)
-    coarse_table = lax.psum(one_hot[:, None] * moments, ("gx", "gy", "gz"))
+    own = one_hot[:, None] * moments
+    parts = lax.all_gather(own, ("gx", "gy", "gz"), axis=0, tiled=False)
+    coarse_table = parts.sum(axis=0)
     far = far_field(coarse_table, weights, middle, cell_coords, fine_dims, coarse_dims)
     result = (summed + far) * alive_mask[None]
     return result.reshape(3, 1, 1, 1, seg_count)

time: 269 us -> 289 us (1.074)
  blocking collectives: 38.6 us -> 64.1 us
  waiting for transfers between devices: 42 us -> 37.1 us
    all_gather x0 -> x1, blocking collectives: none -> 64.1 us  [on_device(): parts = lax.all_gather(own, ('gx', 'gy', 'gz'), axis=0, tiled=False)]
    psum x1 -> x0, blocking collectives: 38.6 us -> none  [on_device(): coarse_table = lax.psum(one_hot[:, None] * moments, ('gx', 'gy', 'gz'))]
  transfers between devices with their start and end apart: 10 -> 10, of which waited for: 7 -> 6; matrix products, arithmetic and copies ran while one was open for 18% -> 16% of each run, Pallas kernels for 0% -> 0%
where the time goes in v1:
time: 289 us; the launch traced here: 285 us
  blocking collectives  64.1 us (22%)
  matrix products  61.3 us (21%)
  local copies, waits for them, and re-layouts  45.8 us (16%)
  other arithmetic  44 us (15%)
  waiting for transfers between devices  37.1 us (13%)
  loops' own time  12.8 us (4%)
  starting transfers between devices  10.3 us (4%)
  between operations  9.99 us (3%)
    all_gather x1, blocking collectives, on_device(): parts = lax.all_gather(own, ('gx', 'gy', 'gz'), axis=0, tiled=False)  64.1 us
    dot_general x32, matrix products, pair_terms(): jnp.dot(target_weight.T, source_weight, precision=HIGHEST, preferred_elem...  60.7 us
    ppermute x6, waiting for transfers between devices, from_behind(): lax.ppermute(shard, axis, [(i, (i + by) % size) for i in range(size)])  35 us
    add x28, other arithmetic, source_step(): inner[0] + forward  34.3 us
    another operation x52, local copies, waits for them, and re-layouts  19.3 us
    another operation x13, loops' own time, on_device(): lax.cond(pair_flags[offset_index] > 0, lambda source=source, source_weigh...  11.6 us
    dynamic_update_slice x20, local copies, waits for them, and re-layouts, target_step(): lax.dynamic_update_slice_in_dim(carried[0], block_force, start, 1)  10.8 us
  transfers between devices with their start and end apart: 10, of which 6 were waited for; matrix products, arithmetic and copies ran while one was open for 16% of the time, Pallas kernels for 0%

profile of v1, /device:TPU:1, one launch (start us, length us, event | category | flops | bytes accessed | tf_op | source)
XLA Modules:
  0.0 285.4 jit_solution(14425362702693000887)
XLA Ops:
  3.7 2.6 collective-permute-start
  7.7 7.9 %while.599 = (s32[]{:T(128)}, f32[3,1024]{1,0:T(4,128)S(1)}, s32[]{:T(128)}, f32[9,1024]{1,0:T(8,128)S(1)}, f32[3,1024]{1,0:T(4,128)S(1)}, /*index=5*/s32[]{:T(1...) while((s32[]{:T(128)}, f32[3,1024]{1,0:T(4,128)S(1)}, ...), condition=%wide.region_7.8_spmd, body=%wide.region_1.7_spmd.sunk | while | flops 34081804 | bytes 199190 | solution.py:103
  7.8 3.8 %while.600 = (s32[]{:T(128)}, f32[3,512]{1,0:T(4,128)S(1)}, s32[]{:T(128)}, f32[9,1024]{1,0:T(8,128)S(1)}, f32[9,512]{1,0:T(8,128)S(1)}, /*index=5*/f32[3,512]{1...) while((s32[]{:T(128)}, f32[3,512]{1,0:T(4,128)S(1)}, ...), condition=%wide.region_6.6_spmd, body=%wide.region_2.5_spmd.sunk | while | flops 34081800 | bytes 127187 | solution.py:98
  11.7 3.8 %while.600 = (s32[]{:T(128)}, f32[3,512]{1,0:T(4,128)S(1)}, s32[]{:T(128)}, f32[9,1024]{1,0:T(8,128)S(1)}, f32[9,512]{1,0:T(8,128)S(1)}, /*index=5*/f32[3,512]{1...) while((s32[]{:T(128)}, f32[3,512]{1,0:T(4,128)S(1)}, ...), condition=%wide.region_6.6_spmd, body=%wide.region_2.5_spmd.sunk | while | flops 34081800 | bytes 127187 | solution.py:98
  15.6 64.1 %all_gather.4 = f32[32,4,117]{2,1,0:T(4,128)S(1)} all-gather(f32[1,4,117]{2,1,0:T(4,128)S(1)} %broadcast_multiply_fusion.14), channel_id=1, replica_groups=mesh['gx'=2,'gy'=4,'gz'=4] {'gx','gy','gz'}, dimensions={0}, use_global_device_ids=true | all-gather | bytes 61776 | tf_op jit(solution)/shard_map/all_gather | solution.py:236
  80.6 3.3 %collective-permute-start.2 = (f32[10,1,3,1,1024]{4,1,3,2,0:T(1,128)S(1)}, f32[10,1,3,1,1024]{4,1,3,2,0:T(1,128)S(1)}, u32[]{:S(2)}, u32[]{:S(2)}) collective-permute-start(f32[10,1,3,1,1024]{4,1,3,2,0:T(1,128)S(1)} %constant_dynamic-update-slice_fusion.14), channel_id=1, source_target_pairs={{1,0},{2,1},{3,2},{0,3},{5,4},{6,5},{7,6},{4,7},{9,8},{10,9},{11,1... | collective-permute-start | bytes 368648 | tf_op jit(solution)/shard_map/ppermute | solution.py:28
  84.1 2.0 collective-permute-done.3
  98.5 11.2 %conditional.16 = (f32[3,1024]{1,0:T(4,128)}, f32[3,1,1024]{2,0,1:T(4,128)}) conditional(s32[]{:T(128)} %bitcast.265, () %tuple.632, (s32[]{:T(128)}, f32[10,1,3,1,1024]{4,1,3,2,0:T(1,128)S(1)}, f32[9,1024]{1,0:T(8,128)S(1)}, f32[3,1024]{1,0:T(4,128)S(1)}) %tuple.1456), branch_computations={%region_44.45_spmd, %region_45.56_spmd} | conditional | flops 35406380 | bytes 787566 | solution.py:188
  101.7 8.0 %while.570 = (s32[]{:T(128)}, f32[3,1024]{1,0:T(4,128)}, f32[3,1024]{1,0:T(4,128)}, s32[]{:T(128)}, f32[9,1024]{1,0:T(8,128)S(1)}, /*index=5*/f32[3,1024]{1,0:T(...) while((s32[]{:T(128)}, f32[3,1024]{1,0:T(4,128)}, ...), condition=%wide.region_55.55_spmd.clone, body=%wide.region_46.54_spmd.clone.sunk | while | flops 35406348 | bytes 361042 | solution.py:103
  101.8 3.3 %while.610 = (s32[]{:T(128)}, f32[3,512]{1,0:T(4,128)S(1)}, f32[3,1024]{1,0:T(4,128)}, s32[]{:T(128)}, f32[9,1024]{1,0:T(8,128)S(1)}, /*index=5*/f32[9,512]{1,0:...) while((s32[]{:T(128)}, f32[3,512]{1,0:T(4,128)S(1)}, ...), condition=%wide.region_54.53_spmd, body=%wide.region_47.52_spmd.sunk | while | flops 35397128 | bytes 155871 | solution.py:98
  105.8 3.3 %while.610 = (s32[]{:T(128)}, f32[3,512]{1,0:T(4,128)S(1)}, f32[3,1024]{1,0:T(4,128)}, s32[]{:T(128)}, f32[9,1024]{1,0:T(8,128)S(1)}, /*index=5*/f32[9,512]{1,0:...) while((s32[]{:T(128)}, f32[3,512]{1,0:T(4,128)S(1)}, ...), condition=%wide.region_54.53_spmd, body=%wide.region_47.52_spmd.sunk | while | flops 35397128 | bytes 155871 | solution.py:98
  109.7 8.1 %conditional.13 = (f32[3,1024]{1,0:T(4,128)}, f32[3,1,3,1024]{3,0,2,1:T(4,128)S(1)}) conditional(s32[]{:T(128)} %bitcast.259, () %tuple.626, (s32[]{:T(128)}, f32[10,1,3,1,1024]{4,1,3,2,0:T(1,128)S(1)}, f32[9,1024]{1,0:T(8,128)S(1)}, f32[3,1024]{1,0:T(4,128)S(1)}) %tuple.1457), branch_computations={%region_8.9_spmd, %region_9.20_spmd} | conditional | flops 35144236 | bytes 840814 | solution.py:188
  112.4 5.4 %while.561 = (s32[]{:T(128)}, f32[3,1024]{1,0:T(4,128)}, f32[3,1024]{1,0:T(4,128)S(1)}, s32[]{:T(128)}, f32[9,1024]{1,0:T(8,128)S(1)}, /*index=5*/f32[3,1024]{1,...) while((s32[]{:T(128)}, f32[3,1024]{1,0:T(4,128)}, ...), condition=%wide.region_19.19_spmd.clone, body=%wide.region_10.18_spmd.clone.sunk | while | flops 35144204 | bytes 365138 | solution.py:103
  112.5 2.0 while.613
  115.2 2.0 while.613
  118.5 17.7 %conditional.14 = (f32[3,1024]{1,0:T(4,128)}, f32[3,1,1024]{2,0,1:T(4,128)}) conditional(s32[]{:T(128)} %bitcast.263, () %tuple.628, (s32[]{:T(128)}, f32[10,1,3,1,1024]{4,1,3,2,0:T(1,128)S(1)}, f32[9,1024]{1,0:T(8,128)S(1)}, f32[3,1024]{1,0:T(4,128)S(1)}) %tuple.1468), branch_computations={%region_20.21_spmd, %region_21.32_spmd} | conditional | flops 35406380 | bytes 787566 | solution.py:188
  121.6 14.6 %while.564 = (s32[]{:T(128)}, f32[3,1024]{1,0:T(4,128)}, f32[3,1024]{1,0:T(4,128)}, s32[]{:T(128)}, f32[9,1024]{1,0:T(8,128)S(1)}, /*index=5*/f32[3,1024]{1,0:T(...) while((s32[]{:T(128)}, f32[3,1024]{1,0:T(4,128)}, ...), condition=%wide.region_31.31_spmd.clone, body=%wide.region_22.30_spmd.clone.sunk | while | flops 35406348 | bytes 361042 | solution.py:103
  121.6 6.7 %while.612 = (s32[]{:T(128)}, f32[3,512]{1,0:T(4,128)S(1)}, f32[3,1024]{1,0:T(4,128)}, s32[]{:T(128)}, f32[9,1024]{1,0:T(8,128)S(1)}, /*index=5*/f32[9,512]{1,0:...) while((s32[]{:T(128)}, f32[3,512]{1,0:T(4,128)S(1)}, ...), condition=%wide.region_30.29_spmd, body=%wide.region_23.28_spmd.sunk | while | flops 35397128 | bytes 155871 | solution.py:98
  128.9 6.6 %while.612 = (s32[]{:T(128)}, f32[3,512]{1,0:T(4,128)S(1)}, f32[3,1024]{1,0:T(4,128)}, s32[]{:T(128)}, f32[9,1024]{1,0:T(8,128)S(1)}, /*index=5*/f32[9,512]{1,0:...) while((s32[]{:T(128)}, f32[3,512]{1,0:T(4,128)S(1)}, ...), condition=%wide.region_30.29_spmd, body=%wide.region_23.28_spmd.sunk | while | flops 35397128 | bytes 155871 | solution.py:98
  136.2 19.0 %conditional.25 = (f32[3,1024]{1,0:T(4,128)}, f32[3,1,1024]{2,0,1:T(4,128)}) conditional(s32[]{:T(128)} %bitcast.274, () %tuple.642, (s32[]{:T(128)}, f32[10,1,3,3,1024]{4,1,3,2,0:T(1,128)}, f32[9,1024]{1,0:T(8,128)S(1)}, f32[3,1024]{1,0:T(4,128)S(1)}) %tuple.1459), branch_computations={%region_152.153_spmd, %region_153.164_spmd} | conditional | flops 35668524 | bytes 1279086 | solution.py:188
  140.3 14.8 %while.597 = (s32[]{:T(128)}, f32[3,1024]{1,0:T(4,128)}, f32[3,1024]{1,0:T(4,128)}, s32[]{:T(128)}, f32[9,1024]{1,0:T(8,128)S(1)}, /*index=5*/f32[3,1024]{1,0:T(...) while((s32[]{:T(128)}, f32[3,1024]{1,0:T(4,128)}, ...), condition=%wide.region_163.163_spmd.clone, body=%wide.region_154.162_spmd.clone.sunk | while | flops 35668492 | bytes 361042 | solution.py:103
  140.4 6.7 %while.601 = (s32[]{:T(128)}, f32[3,512]{1,0:T(4,128)S(1)}, f32[3,1024]{1,0:T(4,128)}, s32[]{:T(128)}, f32[9,1024]{1,0:T(8,128)S(1)}, /*index=5*/f32[9,512]{1,0:...) while((s32[]{:T(128)}, f32[3,512]{1,0:T(4,128)S(1)}, ...), condition=%wide.region_162.161_spmd, body=%wide.region_155.160_spmd.sunk | while | flops 35659272 | bytes 155871 | solution.py:98
  143.9 1.9 fusion.363
  147.8 6.7 %while.601 = (s32[]{:T(128)}, f32[3,512]{1,0:T(4,128)S(1)}, f32[3,1024]{1,0:T(4,128)}, s32[]{:T(128)}, f32[9,1024]{1,0:T(8,128)S(1)}, /*index=5*/f32[9,512]{1,0:...) while((s32[]{:T(128)}, f32[3,512]{1,0:T(4,128)S(1)}, ...), condition=%wide.region_162.161_spmd, body=%wide.region_155.160_spmd.sunk | while | flops 35659272 | bytes 155871 | solution.py:98
  155.2 18.7 %conditional.24 = (f32[3,1024]{1,0:T(4,128)}, f32[3,1,1024]{2,0,1:T(4,128)}) conditional(s32[]{:T(128)} %bitcast.273, () %tuple.641, (s32[]{:T(128)}, f32[10,1,3,3,1024]{4,1,3,2,0:T(1,128)}, f32[9,1024]{1,0:T(8,128)S(1)}, f32[3,1024]{1,0:T(4,128)S(1)}) %tuple.1460), branch_computations={%region_140.141_spmd, %region_141.152_spmd} | conditional | flops 35406380 | bytes 1279086 | solution.py:188
  159.3 14.6 %while.594 = (s32[]{:T(128)}, f32[3,1024]{1,0:T(4,128)}, f32[3,1024]{1,0:T(4,128)}, s32[]{:T(128)}, f32[9,1024]{1,0:T(8,128)S(1)}, /*index=5*/f32[3,1024]{1,0:T(...) while((s32[]{:T(128)}, f32[3,1024]{1,0:T(4,128)}, ...), condition=%wide.region_151.151_spmd.clone, body=%wide.region_142.150_spmd.clone.sunk | while | flops 35406348 | bytes 361042 | solution.py:103
  159.4 6.6 %while.602 = (s32[]{:T(128)}, f32[3,512]{1,0:T(4,128)S(1)}, f32[3,1024]{1,0:T(4,128)}, s32[]{:T(128)}, f32[9,1024]{1,0:T(8,128)S(1)}, /*index=5*/f32[9,512]{1,0:...) while((s32[]{:T(128)}, f32[3,512]{1,0:T(4,128)S(1)}, ...), condition=%wide.region_150.149_spmd, body=%wide.region_143.148_spmd.sunk | while | flops 35397128 | bytes 155871 | solution.py:98
  166.7 6.6 %while.602 = (s32[]{:T(128)}, f32[3,512]{1,0:T(4,128)S(1)}, f32[3,1024]{1,0:T(4,128)}, s32[]{:T(128)}, f32[9,1024]{1,0:T(8,128)S(1)}, /*index=5*/f32[9,512]{1,0:...) while((s32[]{:T(128)}, f32[3,512]{1,0:T(4,128)S(1)}, ...), condition=%wide.region_150.149_spmd, body=%wide.region_143.148_spmd.sunk | while | flops 35397128 | bytes 155871 | solution.py:98
  177.5 18.8 %conditional.20 = (f32[3,1024]{1,0:T(4,128)}, f32[3,1,1024]{2,0,1:T(4,128)}) conditional(s32[]{:T(128)} %bitcast.269, () %tuple.637, (s32[]{:T(128)}, f32[10,1,3,3,1024]{4,1,3,2,0:T(1,128)}, f32[9,1024]{1,0:T(8,128)S(1)}, f32[3,1024]{1,0:T(4,128)S(1)}) %tuple.1464), branch_computations={%region_92.93_spmd, %region_93.104_spmd} | conditional | flops 35406380 | bytes 1279086 | solution.py:188
  181.6 14.6 %while.582 = (s32[]{:T(128)}, f32[3,1024]{1,0:T(4,128)}, f32[3,1024]{1,0:T(4,128)}, s32[]{:T(128)}, f32[9,1024]{1,0:T(8,128)S(1)}, /*index=5*/f32[3,1024]{1,0:T(...) while((s32[]{:T(128)}, f32[3,1024]{1,0:T(4,128)}, ...), condition=%wide.region_103.103_spmd.clone, body=%wide.region_94.102_spmd.clone.sunk | while | flops 35406348 | bytes 361042 | solution.py:103
  181.7 6.7 %while.606 = (s32[]{:T(128)}, f32[3,512]{1,0:T(4,128)S(1)}, f32[3,1024]{1,0:T(4,128)}, s32[]{:T(128)}, f32[9,1024]{1,0:T(8,128)S(1)}, /*index=5*/f32[9,512]{1,0:...) while((s32[]{:T(128)}, f32[3,512]{1,0:T(4,128)S(1)}, ...), condition=%wide.region_102.101_spmd, body=%wide.region_95.100_spmd.sunk | while | flops 35397128 | bytes 155871 | solution.py:98
  189.0 6.7 %while.606 = (s32[]{:T(128)}, f32[3,512]{1,0:T(4,128)S(1)}, f32[3,1024]{1,0:T(4,128)}, s32[]{:T(128)}, f32[9,1024]{1,0:T(8,128)S(1)}, /*index=5*/f32[9,512]{1,0:...) while((s32[]{:T(128)}, f32[3,512]{1,0:T(4,128)S(1)}, ...), condition=%wide.region_102.101_spmd, body=%wide.region_95.100_spmd.sunk | while | flops 35397128 | bytes 155871 | solution.py:98
  196.3 12.2 %conditional.19 = (f32[3,1024]{1,0:T(4,128)}, f32[3,1,1024]{2,0,1:T(4,128)}) conditional(s32[]{:T(128)} %bitcast.268, () %tuple.636, (s32[]{:T(128)}, f32[10,1,3,3,1024]{4,1,3,2,0:T(1,128)}, f32[9,1024]{1,0:T(8,128)S(1)}, f32[3,1024]{1,0:T(4,128)S(1)}) %tuple.1465), branch_computations={%region_80.81_spmd, %region_81.92_spmd} | conditional | flops 35668524 | bytes 1279086 | solution.py:188
  200.4 8.1 %while.579 = (s32[]{:T(128)}, f32[3,1024]{1,0:T(4,128)}, f32[3,1024]{1,0:T(4,128)}, s32[]{:T(128)}, f32[9,1024]{1,0:T(8,128)S(1)}, /*index=5*/f32[3,1024]{1,0:T(...) while((s32[]{:T(128)}, f32[3,1024]{1,0:T(4,128)}, ...), condition=%wide.region_91.91_spmd.clone, body=%wide.region_82.90_spmd.clone.sunk | while | flops 35668492 | bytes 361042 | solution.py:103
  200.5 3.4 %while.607 = (s32[]{:T(128)}, f32[3,512]{1,0:T(4,128)S(1)}, f32[3,1024]{1,0:T(4,128)}, s32[]{:T(128)}, f32[9,1024]{1,0:T(8,128)S(1)}, /*index=5*/f32[9,512]{1,0:...) while((s32[]{:T(128)}, f32[3,512]{1,0:T(4,128)S(1)}, ...), condition=%wide.region_90.89_spmd, body=%wide.region_83.88_spmd.sunk | while | flops 35659272 | bytes 155871 | solution.py:98
  204.5 3.4 %while.607 = (s32[]{:T(128)}, f32[3,512]{1,0:T(4,128)S(1)}, f32[3,1024]{1,0:T(4,128)}, s32[]{:T(128)}, f32[9,1024]{1,0:T(8,128)S(1)}, /*index=5*/f32[9,512]{1,0:...) while((s32[]{:T(128)}, f32[3,512]{1,0:T(4,128)S(1)}, ...), condition=%wide.region_90.89_spmd, body=%wide.region_83.88_spmd.sunk | while | flops 35659272 | bytes 155871 | solution.py:98
  208.5 18.7 %conditional.18 = (f32[3,1024]{1,0:T(4,128)}, f32[3,1,1024]{2,0,1:T(4,128)}) conditional(s32[]{:T(128)} %bitcast.267, () %tuple.635, (s32[]{:T(128)}, f32[10,1,3,3,1024]{4,1,3,2,0:T(1,128)}, f32[9,1024]{1,0:T(8,128)S(1)}, f32[3,1024]{1,0:T(4,128)S(1)}) %tuple.1466), branch_computations={%region_68.69_spmd, %region_69.80_spmd} | conditional | flops 35406380 | bytes 1279086 | solution.py:188
  212.7 14.6 %while.576 = (s32[]{:T(128)}, f32[3,1024]{1,0:T(4,128)}, f32[3,1024]{1,0:T(4,128)}, s32[]{:T(128)}, f32[9,1024]{1,0:T(8,128)S(1)}, /*index=5*/f32[3,1024]{1,0:T(...) while((s32[]{:T(128)}, f32[3,1024]{1,0:T(4,128)}, ...), condition=%wide.region_79.79_spmd.clone, body=%wide.region_70.78_spmd.clone.sunk | while | flops 35406348 | bytes 361042 | solution.py:103
  212.7 6.6 %while.608 = (s32[]{:T(128)}, f32[3,512]{1,0:T(4,128)S(1)}, f32[3,1024]{1,0:T(4,128)}, s32[]{:T(128)}, f32[9,1024]{1,0:T(8,128)S(1)}, /*index=5*/f32[9,512]{1,0:...) while((s32[]{:T(128)}, f32[3,512]{1,0:T(4,128)S(1)}, ...), condition=%wide.region_78.77_spmd, body=%wide.region_71.76_spmd.sunk | while | flops 35397128 | bytes 155871 | solution.py:98
  220.0 6.6 %while.608 = (s32[]{:T(128)}, f32[3,512]{1,0:T(4,128)S(1)}, f32[3,1024]{1,0:T(4,128)}, s32[]{:T(128)}, f32[9,1024]{1,0:T(8,128)S(1)}, /*index=5*/f32[9,512]{1,0:...) while((s32[]{:T(128)}, f32[3,512]{1,0:T(4,128)S(1)}, ...), condition=%wide.region_78.77_spmd, body=%wide.region_71.76_spmd.sunk | while | flops 35397128 | bytes 155871 | solution.py:98
  227.2 12.3 %conditional.17 = (f32[3,1024]{1,0:T(4,128)}, f32[3,1,1024]{2,0,1:T(4,128)}) conditional(s32[]{:T(128)} %bitcast.266, () %tuple.633, (s32[]{:T(128)}, f32[10,1,3,3,1024]{4,1,3,2,0:T(1,128)}, f32[9,1024]{1,0:T(8,128)S(1)}, f32[3,1024]{1,0:T(4,128)S(1)}) %tuple.1467), branch_computations={%region_56.57_spmd, %region_57.68_spmd} | conditional | flops 35668524 | bytes 1279086 | solution.py:188
  231.4 8.1 %while.573 = (s32[]{:T(128)}, f32[3,1024]{1,0:T(4,128)}, f32[3,1024]{1,0:T(4,128)}, s32[]{:T(128)}, f32[9,1024]{1,0:T(8,128)S(1)}, /*index=5*/f32[3,1024]{1,0:T(...) while((s32[]{:T(128)}, f32[3,1024]{1,0:T(4,128)}, ...), condition=%wide.region_67.67_spmd.clone, body=%wide.region_58.66_spmd.clone.sunk | while | flops 35668492 | bytes 361042 | solution.py:103
  231.5 3.4 %while.609 = (s32[]{:T(128)}, f32[3,512]{1,0:T(4,128)S(1)}, f32[3,1024]{1,0:T(4,128)}, s32[]{:T(128)}, f32[9,1024]{1,0:T(8,128)S(1)}, /*index=5*/f32[9,512]{1,0:...) while((s32[]{:T(128)}, f32[3,512]{1,0:T(4,128)S(1)}, ...), condition=%wide.region_66.65_spmd, body=%wide.region_59.64_spmd.sunk | while | flops 35659272 | bytes 155871 | solution.py:98
  235.5 3.4 %while.609 = (s32[]{:T(128)}, f32[3,512]{1,0:T(4,128)S(1)}, f32[3,1024]{1,0:T(4,128)}, s32[]{:T(128)}, f32[9,1024]{1,0:T(8,128)S(1)}, /*index=5*/f32[9,512]{1,0:...) while((s32[]{:T(128)}, f32[3,512]{1,0:T(4,128)S(1)}, ...), condition=%wide.region_66.65_spmd, body=%wide.region_59.64_spmd.sunk | while | flops 35659272 | bytes 155871 | solution.py:98
  242.8 4.6 %collective-permute-done.5 = f32[3,3,3,1024]{3,0,2,1:T(4,128)S(1)} collective-permute-done((f32[3,3,3,1024]{3,0,2,1:T(4,128)S(1)}, f32[3,3,3,1024]{3,0,2,1:T(4,128)S(1)}, u32[]{:S(2)}, u32[]{:S(2)}) %collective-permute-start.5) | collective-permute-done | bytes 110624 | tf_op jit(solution)/shard_map/ppermute | solution.py:35
  249.1 2.8 collective-permute-done.7
  252.0 3.3 %collective-permute-start.9 = (f32[3,1024]{1,0:T(4,128)S(1)}, f32[3,1024]{1,0:T(4,128)S(1)}, u32[]{:S(2)}, u32[]{:S(2)}) collective-permute-start(f32[3,1024]{1,0:T(4,128)S(1)} %get-tuple-element.5495), channel_id=1, source_target_pairs={{0,3},{1,0},{2,1},{3,2},{4,7},{5,4},{6,5},{7,6},{8,11},{9,8},{10,9... | collective-permute-start | bytes 36872 | tf_op jit(solution)/shard_map/ppermute | solution.py:35
  256.4 26.8 %collective-permute-done.9 = f32[3,1024]{1,0:T(4,128)S(1)} collective-permute-done((f32[3,1024]{1,0:T(4,128)S(1)}, f32[3,1024]{1,0:T(4,128)S(1)}, u32[]{:S(2)}, u32[]{:S(2)}) %collective-permute-start.9) | collective-permute-done | bytes 12320 | tf_op jit(solution)/shard_map/ppermute | solution.py:35
  (421 shorter events, 156.0 us)
Async XLA Ops:
  0.7 2.2 copy-start.22
  2.1 0.7 copy-start.19
  2.8 0.7 copy-start.15
  2.8 0.7 copy-start.21
  3.6 76.9 %collective-permute-start.1 = (f32[10,1,1,1,1024]{4,1,3,2,0:T(1,128)S(1)}, f32[10,1,1,1,1024]{4,1,3,2,0:T(1,128)S(1)}, u32[]{:S(2)}, u32[]{:S(2)}) collective-permute-start(f32[10,1,1,1,1024]{4,1,3,2,0:T(1,128)S(1)} %reshape.982), channel_id=1, source_target_pairs={{4,0},{8,4},{12,8},{0,12},{5,1},{9,5},{13,9},{1,13},{6,2},{10,6},{... | collective-permute-start | bytes 122888 | tf_op jit(solution)/shard_map/ppermute | solution.py:28
  3.7 76.8 %collective-permute-start = (f32[10,1,1,1,1024]{4,1,3,2,0:T(1,128)S(1)}, f32[10,1,1,1,1024]{4,1,3,2,0:T(1,128)S(1)}, u32[]{:S(2)}, u32[]{:S(2)}) collective-permute-start(f32[10,1,1,1,1024]{4,1,3,2,0:T(1,128)S(1)} %reshape.982), channel_id=1, source_target_pairs={{0,4},{4,8},{8,12},{12,0},{1,5},{5,9},{9,13},{13,1},{2,6},{6,10},{... | collective-permute-start | bytes 122888 | tf_op jit(solution)/shard_map/ppermute | solution.py:25
  15.6 64.2 %copy-start.16 = (f32[3,1024]{1,0:T(4,128)}, f32[3,1024]{1,0:T(4,128)S(1)}, u32[]{:S(2)}) copy-start(f32[3,1024]{1,0:T(4,128)S(1)} %get-tuple-element.4222) | copy-start | bytes 36868
  80.4 16.2 %copy-start.7 = (f32[1,4,1024]{2,1,0:T(4,128)}, f32[1,4,1024]{2,1,0:T(4,128)S(1)}, u32[]{:S(2)}) copy-start(f32[1,4,1024]{2,1,0:T(4,128)S(1)} %get-tuple-element.5525) | copy-start | bytes 49156
  80.4 16.2 %copy-start.9 = (f32[1,4,1024]{2,1,0:T(4,128)}, f32[1,4,1024]{2,1,0:T(4,128)S(1)}, u32[]{:S(2)}) copy-start(f32[1,4,1024]{2,1,0:T(4,128)S(1)} %get-tuple-element.5526) | copy-start | bytes 49156
  80.4 16.1 %copy-start.5 = (f32[1,4,1024]{2,1,0:T(4,128)}, f32[1,4,1024]{2,1,0:T(4,128)S(1)}, u32[]{:S(2)}) copy-start(f32[1,4,1024]{2,1,0:T(4,128)S(1)} %add_add_fusion.2) | copy-start | bytes 49156
  80.5 5.6 %collective-permute-start.3 = (f32[10,1,3,1,1024]{4,1,3,2,0:T(1,128)S(1)}, f32[10,1,3,1,1024]{4,1,3,2,0:T(1,128)S(1)}, u32[]{:S(2)}, u32[]{:S(2)}) collective-permute-start(f32[10,1,3,1,1024]{4,1,3,2,0:T(1,128)S(1)} %constant_dynamic-update-slice_fusion.14), channel_id=1, source_target_pairs={{0,1},{1,2},{2,3},{3,0},{4,5},{5,6},{6,7},{7,4},{8,9},{9,10},{10,1... | collective-permute-start | bytes 368648 | tf_op jit(solution)/shard_map/ppermute | solution.py:25
  80.6 5.5 %collective-permute-start.2 = (f32[10,1,3,1,1024]{4,1,3,2,0:T(1,128)S(1)}, f32[10,1,3,1,1024]{4,1,3,2,0:T(1,128)S(1)}, u32[]{:S(2)}, u32[]{:S(2)}) collective-permute-start(f32[10,1,3,1,1024]{4,1,3,2,0:T(1,128)S(1)} %constant_dynamic-update-slice_fusion.14), channel_id=1, source_target_pairs={{1,0},{2,1},{3,2},{0,3},{5,4},{6,5},{7,6},{4,7},{9,8},{10,9},{11,1... | collective-permute-start | bytes 368648 | tf_op jit(solution)/shard_map/ppermute | solution.py:28
  84.0 12.6 %copy-start = (f32[1024,4,13]{0,1,2:T(4,128)}, f32[1024,4,13]{0,1,2:T(4,128)S(1)}, u32[]{:S(2)}) copy-start(f32[1024,4,13]{0,1,2:T(4,128)S(1)} %copy.70) | copy-start | bytes 638980
  84.1 12.5 %copy-start.3 = (f32[3,4,1024]{2,1,0:T(4,128)}, f32[3,4,1024]{2,1,0:T(4,128)S(1)}, u32[]{:S(2)}) copy-start(f32[3,4,1024]{2,1,0:T(4,128)S(1)} %multiply_reduce_fusion) | copy-start | bytes 147460
  86.1 1.1 copy-start.1
  87.2 49.0 %collective-permute-start.4 = (f32[10,1,3,3,1024]{4,1,3,2,0:T(1,128)}, f32[10,1,3,3,1024]{4,1,3,2,0:T(1,128)}, u32[]{:S(2)}, u32[]{:S(2)}) collective-permute-start(f32[10,1,3,3,1024]{4,1,3,2,0:T(1,128)} %pad_maximum_fusion), channel_id=1, source_target_pairs={{0,16},{16,0},{1,17},{17,1},{2,18},{18,2},{3,19},{19,3},{4,20},{20... | collective-permute-start | bytes 1105928 | tf_op jit(solution)/shard_map/ppermute | solution.py:35
  96.6 0.7 copy-start.13
  109.7 8.1 %copy-start.2 = (f32[10,1,3,1,1024]{4,1,3,2,0:T(1,128)S(1)}, f32[10,1,3,1,1024]{4,1,3,2,0:T(1,128)}, u32[]{:S(2)}) copy-start(f32[10,1,3,1,1024]{4,1,3,2,0:T(1,128)} %copy-done.1) | copy-start | bytes 368644
  117.8 0.6 copy-start.11
  241.9 5.5 %collective-permute-start.5 = (f32[3,3,3,1024]{3,0,2,1:T(4,128)S(1)}, f32[3,3,3,1024]{3,0,2,1:T(4,128)S(1)}, u32[]{:S(2)}, u32[]{:S(2)}) collective-permute-start(f32[3,3,3,1024]{3,0,2,1:T(4,128)S(1)} %pad_maximum_fusion.1), channel_id=1, source_target_pairs={{0,16},{16,0},{1,17},{17,1},{2,18},{18,2},{3,19},{19,3},{4,20},{20... | collective-permute-start | bytes 331784 | tf_op jit(solution)/shard_map/ppermute | solution.py:35
  242.0 5.4 %copy-start.12 = (f32[3,1,3,1024]{3,0,2,1:T(4,128)S(1)}, f32[3,1,3,1024]{3,0,2,1:T(4,128)}, u32[]{:S(2)}) copy-start(f32[3,1,3,1024]{3,0,2,1:T(4,128)} %copy-done.11) | copy-start | bytes 110596
  242.7 4.6 %copy-start.23 = (f32[3]{0:T(128)S(1)}, f32[3]{0:T(128)}, u32[]{:S(2)}) copy-start(f32[3]{0:T(128)} %pad.105.clone) | copy-start | bytes 40
  247.5 1.0 copy-start.14
  247.5 1.6 collective-permute-start.6
  247.6 4.3 %collective-permute-start.7 = (f32[3,3,1024]{2,0,1:T(4,128)S(1)}, f32[3,3,1024]{2,0,1:T(4,128)S(1)}, u32[]{:S(2)}, u32[]{:S(2)}) collective-permute-start(f32[3,3,1024]{2,0,1:T(4,128)S(1)} %get-tuple-element.5493), channel_id=1, source_target_pairs={{0,12},{4,0},{8,4},{12,8},{1,13},{5,1},{9,5},{13,9},{2,14},{6,2},{... | collective-permute-start | bytes 110600 | tf_op jit(solution)/shard_map/ppermute | solution.py:35
  251.9 3.4 %copy-start.8 = (f32[1,4,1024]{2,1,0:T(4,128)S(1)}, f32[1,4,1024]{2,1,0:T(4,128)}, u32[]{:S(2)}) copy-start(f32[1,4,1024]{2,1,0:T(4,128)} %copy-done.7) | copy-start | bytes 49156
  251.9 3.4 %copy-start.10 = (f32[1,4,1024]{2,1,0:T(4,128)S(1)}, f32[1,4,1024]{2,1,0:T(4,128)}, u32[]{:S(2)}) copy-start(f32[1,4,1024]{2,1,0:T(4,128)} %copy-done.9) | copy-start | bytes 49156
  251.9 3.4 %copy-start.18 = (f32[4,1024]{1,0:T(4,128)S(1)}, f32[4,1024]{1,0:T(4,128)}, u32[]{:S(2)}) copy-start(f32[4,1024]{1,0:T(4,128)} %fusion.244) | copy-start | bytes 49156
  251.9 3.4 %copy-start.4 = (f32[3,4,1024]{2,1,0:T(4,128)S(1)}, f32[3,4,1024]{2,1,0:T(4,128)}, u32[]{:S(2)}) copy-start(f32[3,4,1024]{2,1,0:T(4,128)} %copy-done.3) | copy-start | bytes 147460
  251.9 3.4 %copy-start.6 = (f32[1,4,1024]{2,1,0:T(4,128)S(1)}, f32[1,4,1024]{2,1,0:T(4,128)}, u32[]{:S(2)}) copy-start(f32[1,4,1024]{2,1,0:T(4,128)} %copy-done.5) | copy-start | bytes 49156
  252.0 4.4 %collective-permute-start.8 = (f32[3,1024]{1,0:T(4,128)S(1)}, f32[3,1024]{1,0:T(4,128)S(1)}, u32[]{:S(2)}, u32[]{:S(2)}) collective-permute-start(f32[3,1024]{1,0:T(4,128)S(1)} %get-tuple-element.5494), channel_id=1, source_target_pairs={{0,1},{1,2},{2,3},{3,0},{4,5},{5,6},{6,7},{7,4},{8,9},{9,10},{10,1... | collective-permute-start | bytes 36872 | tf_op jit(solution)/shard_map/ppermute | solution.py:35
  252.0 31.1 %collective-permute-start.9 = (f32[3,1024]{1,0:T(4,128)S(1)}, f32[3,1024]{1,0:T(4,128)S(1)}, u32[]{:S(2)}, u32[]{:S(2)}) collective-permute-start(f32[3,1024]{1,0:T(4,128)S(1)} %get-tuple-element.5495), channel_id=1, source_target_pairs={{0,3},{1,0},{2,1},{3,2},{4,7},{5,4},{6,5},{7,6},{8,11},{9,8},{10,9... | collective-permute-start | bytes 36872 | tf_op jit(solution)/shard_map/ppermute | solution.py:35
  256.2 27.0 %copy-start.17 = (f32[3,1024]{1,0:T(4,128)S(1)}, f32[3,1024]{1,0:T(4,128)}, u32[]{:S(2)}) copy-start(f32[3,1024]{1,0:T(4,128)} %copy-done.16) | copy-start | bytes 36868
  283.2 0.7 copy-start.20
